TPU v7x, 32 devices: a whole 2x2x4 slice. The times are simulated.
32 devices in a mesh: ctx: 4 (over z), exp: 4 (over y, x), head: 2 (over core).
Axes of the slice: x: 2, y: 2, z: 4, core: 2. Of those that a mesh axis runs over, the one named last changes fastest.
Arguments:
- queries: bfloat16 [2048, 2048], P(('ctx', 'exp'), 'head'), may hold values from -6 to 6
- keys: bfloat16 [2048, 256], P(('ctx', 'exp'), 'head'), may hold values from -6 to 6
- values: bfloat16 [2048, 256], P(('ctx', 'exp'), 'head'), may hold values from -12 to 12
- residual: bfloat16 [2048, 2880], P(('ctx', 'exp', 'head')), may hold values from -48 to 48
- out_projection: bfloat16 [2048, 2880], P('head', 'exp'), may hold values from -0.125 to 0.125
- norm_gain: float32 [2880], replicated, may hold values from 0.25 to 1.75
- route_ids: int32 [2048, 4], P(('ctx', 'exp', 'head')), may hold values from 0 to 7, all different within a row; in each aligned block of 64 rows (0 to 63, 64 to 127, ...) at most 64 rows name the same one
- route_weights: float32 [2048, 4], P(('ctx', 'exp', 'head')), may hold values from 0.05 to 1
- w_gate: bfloat16 [8, 2880, 1536], P(('ctx', 'head'), None, 'exp'), may hold values from -0.109375 to 0.109375
- w_up: bfloat16 [8, 2880, 1536], P(('ctx', 'head'), None, 'exp'), may hold values from -0.109375 to 0.109375
- w_down: bfloat16 [8, 1536, 2880], P(('ctx', 'head'), 'exp'), may hold values from -0.15625 to 0.15625
Outputs:
- mixed: bfloat16 [2048, 2880], P(('ctx', 'exp', 'head'))
Inputs may be any that keep to these rules, and one draw needn't show every extreme that they name: `route_ids`: each row names 4 different experts. In the rows of one device (aligned blocks of 64 rows) no expert is named by more than 64 rows, a bound that some block reaches.
All inputs are finite; a program needn't handle non-finite values.
Results may differ from a plain program's by a relative error of at most 0.0037.
Values may be sent and summed in bfloat16 or wider, within the bound.
No kernel may reach another device: no remote copies, remote signals or barrier semaphores. Data moves between devices by JAX's collectives and lax.ppermute only.
A program may use at most 128 MiB of HBM per device.

v0:
```python
import jax
import jax.numpy as jnp
from jax import lax
from jax.sharding import PartitionSpec as P

D = 2880
QUERY_HEADS = 32
KEY_VALUE_HEADS = 4
HEAD_DIMENSION = 64
BAND_WIDTH_KEYS = 128
TOP = 4
EPSILON = 1e-05
SLOPE = 1.702


def from_behind(x, axis, by):
    devices = lax.axis_size(axis)
    pairs = [(i, i + by) for i in range(devices) if 0 <= i + by < devices]
    return lax.ppermute(x, axis, pairs)


def attend_band(
    queries, concatenated_keys, concatenated_values, window, head_size, group, anchor_position
):
    tokens = queries.shape[0]
    block = min(tokens, 512)
    count = tokens // block
    heads = queries.shape[1] // head_size
    kv_heads = heads // group
    scale = head_size ** (-0.5)

    def one_block(index):
        begin = index * block
        query_part = queries.reshape(block, kv_heads, group, head_size)
        key_part = concatenated_keys.reshape(block + window, kv_heads, head_size)
        value_part = concatenated_values.reshape(block + window, kv_heads, head_size)
        scores = (
            jnp.einsum("qgjd,kgd->gjqk", query_part, key_part, preferred_element_type=jnp.float32)
            * scale
        )
        query_pos = anchor_position + begin + jnp.arange(block, dtype=jnp.int32)
        key_pos = anchor_position - window + begin + jnp.arange(block + window, dtype=jnp.int32)
        distance = query_pos[:, None] - key_pos[None, :]
        allowed = (distance >= 0) & (distance < window) & (key_pos[None, :] >= 0)
        scores = jnp.where(allowed, scores, -jnp.inf)
        highest = jnp.max(scores, axis=-1, keepdims=True)
        weights = jnp.exp(scores - highest)
        weights = (weights / jnp.sum(weights, axis=-1, keepdims=True)).astype(jnp.bfloat16)
        result = jnp.einsum(
            "gjqk,kgd->qgjd", weights, value_part, preferred_element_type=jnp.float32
        )
        return result.astype(jnp.bfloat16).reshape(block, heads * head_size)

    outputs = lax.map(one_block, jnp.arange(count, dtype=jnp.int32))
    return outputs.reshape(tokens, heads * head_size)


def expert_rows(inputs, gate_slice, up_slice, down_slice):
    gate = jnp.dot(inputs, gate_slice, preferred_element_type=jnp.float32)
    upward = jnp.dot(inputs, up_slice, preferred_element_type=jnp.float32)
    active = ((upward + 1.0) * gate * jax.nn.sigmoid(SLOPE * gate)).astype(jnp.bfloat16)
    return jnp.dot(active, down_slice, preferred_element_type=jnp.float32)


def local(
    queries,
    keys,
    values,
    residual,
    out_projection,
    norm_gain,
    route_ids,
    route_weights,
    w_gate,
    w_up,
    w_down,
):
    tokens = queries.shape[0]
    key_band_extent = keys.shape[1]
    stacked = jnp.concatenate([keys, values], axis=1)
    prior = from_behind(stacked, ("ctx", "exp"), 1)
    joined_heads = jnp.concatenate([prior, stacked], axis=0)
    anchor_position = lax.axis_index(("ctx", "exp")) * tokens
    attended_rows = attend_band(
        queries,
        joined_heads[:, :key_band_extent],
        joined_heads[:, key_band_extent:],
        BAND_WIDTH_KEYS,
        HEAD_DIMENSION,
        QUERY_HEADS // KEY_VALUE_HEADS,
        anchor_position,
    )
    partial_sum = jnp.dot(
        attended_rows,
        lax.all_gather(out_projection, "exp", axis=1, tiled=True),
        preferred_element_type=jnp.float32,
    )
    attn_out = lax.psum_scatter(partial_sum, "head", scatter_dimension=0, tiled=True)
    hidden_state = residual.astype(jnp.float32) + attn_out
    mean_square = jnp.mean(hidden_state * hidden_state, axis=1, keepdims=True)
    normed = (hidden_state * lax.rsqrt(mean_square + EPSILON) * norm_gain[None, :]).astype(
        jnp.bfloat16
    )
    local_rows = normed.shape[0]
    experts = lax.axis_size("ctx") * lax.axis_size("head")
    capacity = max(2, TOP * tokens // experts)
    flat_ids = route_ids.reshape(-1)
    one_hot = (flat_ids[:, None] == jnp.arange(experts, dtype=jnp.int32)[None, :]).astype(jnp.int32)
    earlier = jnp.cumsum(one_hot, axis=0) - one_hot
    rank = jnp.sum(earlier * one_hot, axis=1)
    slot = flat_ids * capacity + rank
    outgoing = (
        jnp.zeros((experts * capacity, D), jnp.bfloat16)
        .at[slot]
        .set(jnp.repeat(normed, TOP, axis=0))
    )
    outgoing = outgoing.reshape(experts, capacity, D)
    arrived = lax.all_to_all(outgoing, ("ctx", "head"), split_axis=0, concat_axis=0, tiled=True)
    pooled = lax.all_gather(arrived, "exp", axis=0, tiled=True)
    partial_rows = expert_rows(
        pooled.reshape(experts * lax.axis_size("exp") * capacity, D), w_gate[0], w_up[0], w_down[0]
    )
    summed = lax.psum_scatter(
        partial_rows.reshape(experts * lax.axis_size("exp"), capacity, D),
        "exp",
        scatter_dimension=0,
        tiled=True,
    ).astype(jnp.bfloat16)
    returned = lax.all_to_all(summed, ("ctx", "head"), split_axis=0, concat_axis=0, tiled=True)
    flat_back = returned.reshape(experts * capacity, D)
    picked = flat_back[slot].astype(jnp.float32).reshape(local_rows, TOP, D)
    moe = jnp.sum(picked * route_weights[:, :, None], axis=1)
    return (hidden_state + moe).astype(jnp.bfloat16)


def solution(mesh):
    return jax.shard_map(
        local,
        mesh=mesh,
        in_specs=(
            P(("ctx", "exp"), "head"),
            P(("ctx", "exp"), "head"),
            P(("ctx", "exp"), "head"),
            P(("ctx", "exp", "head"), None),
            P("head", "exp"),
            P(),
            P(("ctx", "exp", "head"), None),
            P(("ctx", "exp", "head"), None),
            P(("ctx", "head"), None, "exp"),
            P(("ctx", "head"), None, "exp"),
            P(("ctx", "head"), "exp", None),
        ),
        out_specs=P(("ctx", "exp", "head"), None),
        check_vma=False,
    )
```

profile of v0, /device:TPU:0, one launch (start us, length us, event | category | flops | bytes accessed | tf_op | source)
XLA Modules:
  0.0 637.0 jit_solution(17359367700430694004)
XLA Ops:
  6.5 0.0 copy-start
  6.5 0.0 all-gather.3.cloned.1.call-start
  6.5 0.7 all-gather.3.cloned.1.call-update
  7.3 0.0 reduce-scatter.3.cloned.1.call-start
  7.3 0.8 constant_dynamic-update-slice_fusion.1
  8.1 0.8 constant_dynamic-update-slice_fusion
  8.8 4.9 collective-permute-start
  13.8 0.1 fusion.15
  13.9 1.1 copy.27
  15.0 0.6 collective-permute-done
  15.6 0.1 copy.26
  15.7 0.1 copy.25
  15.8 0.8 fusion.26
  16.6 1.1 convolution_convert_fusion
  17.7 61.0 %all-gather.3.cloned.1.call-done = bf16[1024,2880]{0,1:T(8,128)(2,1)} async-done(((bf16[1024,720]{0,1:T(8,128)(2,1)}), bf16[1024,2880]{0,1:T(8,128)(2,1)}) %all-gather.3.cloned.1.call-update) | async-done | bytes 5898256 | tf_op jit(solution)/shard_map/all_gather | solution.py:95
  78.7 0.0 copy-start.5
  78.7 0.0 copy-start.3
  78.7 6.0 fusion.27
  84.7 0.0 copy-start.4
  84.7 0.0 reduce-scatter.3.cloned.1.call-update
  84.7 0.0 all-gather.5.cloned.1.call-start
  84.8 0.0 copy-done.5
  84.8 0.1 copy.30
  84.9 0.1 eq.29
  85.0 0.1 eq.25
  85.1 0.6 reduce-window.6
  85.7 0.2 slice_reduce_fusion
  85.9 0.1 copy.29
  86.0 0.1 mul.79
  86.1 0.1 fusion.18
  86.2 7.6 %reduce-scatter.3.cloned.1.call-done = f32[64,2880]{1,0:T(8,128)} async-done(((f32[128,2880]{1,0:T(8,128)}), f32[64,2880]{1,0:T(8,128)}) %reduce-scatter.3.cloned.1.call-update) | async-done | bytes 737296 | tf_op jit(solution)/shard_map/reduce_scatter | solution.py:98
  93.8 0.0 copy-done.3
  93.8 1.3 multiply_reduce_fusion.1
  95.2 0.0 copy-done.4
  95.2 1.3 multiply_convert_fusion.1
  96.4 1.5 broadcast_in_dim.38
  98.0 3.6 reshape.129
  101.5 5.6 scatter_custom_fusion
  107.1 73.8 %all_to_all.10 = bf16[8,64,2880]{2,1,0:T(8,128)(2,1)} all-to-all(bf16[8,64,2880]{2,1,0:T(8,128)(2,1)} %bitcast.60), channel_id=1, replica_groups=mesh['ctx'=4,'exp'=4,'head'=2] {'ctx','head'}, dimensions={0} | all-to-all | bytes 5898240 | tf_op jit(solution)/shard_map/all_to_all | solution.py:118
  180.9 0.0 all-gather.5.cloned.1.call-update
  180.9 0.2 reduce-scatter.5.cloned.1.call-start
  181.1 116.8 %all-gather.5.cloned.1.call-done = bf16[32,64,2880]{2,1,0:T(8,128)(2,1)} async-done(((bf16[8,64,2880]{2,1,0:T(8,128)(2,1)}), bf16[32,64,2880]{2,1,0:T(8,128)(2,1)}) %all-gather.5.cloned.1.call-update) | async-done | bytes 11796496 | tf_op jit(solution)/shard_map/all_gather | solution.py:119
  298.0 0.0 copy-start.7
  298.0 0.0 copy-start.8
  298.0 10.6 %fusion.3 = f32[2048,384]{1,0:T(8,128)S(1)} fusion(bf16[2048,2880]{1,0:T(8,128)(2,1)} %bitcast.71, bf16[1,2880,384]{2,1,0:T(8,128)(2,1)} %param.19), kind=kOutput, calls=%fused_computation.7 | convolution fusion | flops 4529848320 | bytes 17154048 | tf_op jit(solution)/shard_map/dot_general | solution.py:59
  308.6 0.0 copy-done.7
  308.6 0.0 copy-done.8
  308.6 7.3 %multiply_convert_fusion = bf16[2048,384]{1,0:T(8,128)(2,1)S(1)} fusion(f32[2048,384]{1,0:T(8,128)S(1)} %fusion.3, bf16[2048,2880]{1,0:T(8,128)(2,1)S(1)} %bitcast.72, bf16[1,2880,384]{2,1,0:T(8,128)(2,1)S(1)} %copy-done.8), kind=kOutput, calls=%fused_computation.3 | convolution fusion | flops 4536139776 | bytes 18726912 | tf_op jit(solution)/shard_map/dot_general | solution.py:60
  315.9 0.0 copy-done
  315.9 11.4 %fusion.1 = f32[32,64,2880]{2,1,0:T(8,128)} fusion(bf16[32,64,384]{2,1,0:T(8,128)(2,1)S(1)} %bitcast.61, bf16[1,384,2880]{1,2,0:T(8,128)(2,1)S(1)} %copy-done), kind=kOutput, calls=%fused_computation.5 | convolution fusion | flops 4529848320 | bytes 27377664 | tf_op jit(solution)/shard_map/dot_general | solution.py:62
  327.3 0.0 reduce-scatter.5.cloned.1.call-update
  327.3 213.4 %reduce-scatter.5.cloned.1.call-done = f32[8,64,2880]{2,1,0:T(8,128)} async-done(((f32[32,64,2880]{2,1,0:T(8,128)}), f32[8,64,2880]{2,1,0:T(8,128)}) %reduce-scatter.5.cloned.1.call-update) | async-done | bytes 5898256 | tf_op jit(solution)/shard_map/reduce_scatter | solution.py:123
  540.7 4.8 convert_element_type.48
  545.4 0.0 copy-start.6
  545.4 4.7 all-to-all-start.1
  550.2 0.0 copy-done.6
  550.2 0.1 copy.32
  550.3 68.6 %all-to-all-done.1 = bf16[8,64,2880]{2,1,0:T(8,128)(2,1)S(1)} async-done(((bf16[8,64,2880]{2,1,0:T(8,128)(2,1)}), bf16[8,64,2880]{2,1,0:T(8,128)(2,1)S(1)}, u32[]{:S(2)}, u32[]{:S(2)}) %all-to-all-start.1) | async-done | bytes 2949152 | tf_op jit(solution)/shard_map/all_to_all | solution.py:129
  618.9 2.7 gather_fusion
  621.5 4.1 reshape.116
  625.6 4.0 multiply_reduce_fusion
  629.6 0.0 copy-done.2
  629.6 0.9 add_convert_fusion
  630.5 0.0 copy-done.1
  (13 shorter events, 0.1 us)
Async XLA Ops:
  6.5 309.3 %copy-start = (bf16[1,384,2880]{1,2,0:T(8,128)(2,1)S(1)}, bf16[1,384,2880]{1,2,0:T(8,128)(2,1)}, u32[]{:S(2)}) copy-start(bf16[1,384,2880]{1,2,0:T(8,128)(2,1)} %param.21) | copy-start | bytes 6635524
  6.5 72.2 %all-gather.3.cloned.1.call-start = ((), (), s32[]{:S(2)}) async-start(), calls=%async_computation.4 | async-start | bytes 7372800 | tf_op jit(solution)/shard_map/all_gather | solution.py:95
  7.3 86.6 %reduce-scatter.3.cloned.1.call-start = ((), (), s32[]{:S(2)}) async-start(), calls=%async_computation.5 | async-start | bytes 2260992 | tf_op jit(solution)/shard_map/reduce_scatter | solution.py:98
  8.8 6.8 %collective-permute-start = (bf16[128,256]{1,0:T(8,128)(2,1)S(1)}, bf16[128,256]{1,0:T(8,128)(2,1)S(1)}, u32[]{:S(2)}, u32[]{:S(2)}) collective-permute-start(bf16[128,256]{1,0:T(8,128)(2,1)S(1)} %constant_dynamic-update-slice_fusion), channel_id=1, source_target_pairs={{0,2},{2,4},{4,6},{6,8},{8,10},{10,12},{12,14},{14,16},{16,18},{18... | collective-permute-start | bytes 196616 | tf_op jit(solution)/shard_map/ppermute | solution.py:19
  78.7 6.1 copy-start.5
  78.7 15.1 %copy-start.3 = (bf16[64,2880]{1,0:T(8,128)(2,1)S(1)}, bf16[64,2880]{1,0:T(8,128)(2,1)}, u32[]{:S(2)}) copy-start(bf16[64,2880]{1,0:T(8,128)(2,1)} %param.14) | copy-start | bytes 1105924
  84.7 10.5 %copy-start.4 = (f32[2880]{0:T(1024)S(1)}, f32[2880]{0:T(1024)}, u32[]{:S(2)}) copy-start(f32[2880]{0:T(1024)} %param.16) | copy-start | bytes 34564
  84.7 213.3 %all-gather.5.cloned.1.call-start = ((), (), s32[]{:S(2)}) async-start(), calls=%async_computation.6 | async-start | bytes 15073280 | tf_op jit(solution)/shard_map/all_gather | solution.py:119
  180.9 359.7 %reduce-scatter.5.cloned.1.call-start = ((), (), s32[]{:S(2)}) async-start(), calls=%async_computation.7 | async-start | bytes 30146560 | tf_op jit(solution)/shard_map/reduce_scatter | solution.py:123
  298.0 10.6 %copy-start.7 = (bf16[32,64,2880]{2,1,0:T(8,128)(2,1)S(1)}, bf16[32,64,2880]{2,1,0:T(8,128)(2,1)}, u32[]{:S(2)}) copy-start(bf16[32,64,2880]{2,1,0:T(8,128)(2,1)} %all-gather.5.cloned.1.call-done) | copy-start | bytes 35389444
  298.0 10.6 %copy-start.8 = (bf16[1,2880,384]{2,1,0:T(8,128)(2,1)S(1)}, bf16[1,2880,384]{2,1,0:T(8,128)(2,1)}, u32[]{:S(2)}) copy-start(bf16[1,2880,384]{2,1,0:T(8,128)(2,1)} %param.20) | copy-start | bytes 6635524
  545.4 4.7 copy-start.6
  545.4 73.4 %all-to-all-start.1 = ((bf16[8,64,2880]{2,1,0:T(8,128)(2,1)}), bf16[8,64,2880]{2,1,0:T(8,128)(2,1)S(1)}, u32[]{:S(2)}, u32[]{:S(2)}) async-start(bf16[8,64,2880]{2,1,0:T(8,128)(2,1)} %convert_element_type.48), calls=%async_computation.3 | async-start | bytes 6029312 | tf_op jit(solution)/shard_map/all_to_all | solution.py:129
  621.5 8.9 %copy-start.1 = (bf16[1,384,2880]{1,2,0:T(8,128)(2,1)S(1)}, bf16[1,384,2880]{1,2,0:T(8,128)(2,1)}, u32[]{:S(2)}) copy-start(bf16[1,384,2880]{1,2,0:T(8,128)(2,1)} %param.21) | copy-start | bytes 6635524
  625.6 4.0 copy-start.2
Sparse Core Ops, SparseCore 0:
  9.2 69.4 all-gather.2
  84.8 8.9 reduce-scatter.2
  181.0 116.8 all-gather.4
  327.4 213.2 reduce-scatter.4
where the time goes:
time: 638 us; the launch traced here: 637 us
  waiting for transfers between devices  469 us (74%)
  blocking collectives  73.8 us (12%)
  matrix products  37.1 us (6%)
  local copies, waits for them, and re-layouts  21.2 us (3%)
  between operations  13.3 us (2%)
  other arithmetic  13.1 us (2%)
  starting transfers between devices  9.91 us (2%)
    reduce_scatter x1, waiting for transfers between devices, local(): lax.psum_scatter(partial_rows.reshape(experts * lax.axis_size('exp'), cap...  213 us
    all_gather x1, waiting for transfers between devices, local(): pooled = lax.all_gather(arrived, 'exp', axis=0, tiled=True)  117 us
    all_to_all x1, blocking collectives, local(): lax.all_to_all(outgoing, ('ctx', 'head'), split_axis=0, concat_axis=0, ti...  73.8 us
    all_to_all x1, waiting for transfers between devices, local(): lax.all_to_all(summed, ('ctx', 'head'), split_axis=0, concat_axis=0, tile...  68.6 us
    all_gather x1, waiting for transfers between devices, local(): lax.all_gather(out_projection, 'exp', axis=1, tiled=True)  61 us
  transfers between devices with their start and end apart: 6, of which 6 were waited for; matrix products, arithmetic and copies ran while one was open for 1% of the time, Pallas kernels for 0%

commit v1 on v0

--- a/solution.py
+++ b/solution.py
@@ -116,7 +116,16 @@
     )
     outgoing = outgoing.reshape(experts, capacity, D)
     arrived = lax.all_to_all(outgoing, ("ctx", "head"), split_axis=0, concat_axis=0, tiled=True)
-    pooled = lax.all_gather(arrived, "exp", axis=0, tiled=True)
+    length, index_2, extent = (lax.axis_size("exp"), lax.axis_index("exp"), arrived.shape[0])
+    ahead = [(i_2, (i_2 + 1) % length) for i_2 in range(length)]
+    out = jnp.zeros((*arrived.shape[:0], length * extent, *arrived.shape[0 + 1 :]), arrived.dtype)
+    held = arrived
+    for step in range(length):
+        holder = (index_2 - step) % length
+        out = lax.dynamic_update_slice_in_dim(out, held, holder * extent, axis=0)
+        if step < length - 1:
+            held = lax.ppermute(held, "exp", ahead)
+    pooled = out
     partial_rows = expert_rows(
         pooled.reshape(experts * lax.axis_size("exp") * capacity, D), w_gate[0], w_up[0], w_down[0]
     )

time: 638 us -> 732 us (1.15)
  waiting for transfers between devices: 469 us -> 536 us
  local copies, waits for them, and re-layouts: 21.2 us -> 46.3 us
    ppermute x0 -> x3, waiting for transfers between devices: none -> 184 us  [local(): held = lax.ppermute(held, 'exp', ahead)]
    all_gather x1 -> x0, waiting for transfers between devices: 117 us -> none  [local(): pooled = lax.all_gather(arrived, 'exp', axis=0, tiled=True)]
    dynamic_update_slice x0 -> x4, local copies, waits for them, and re-layouts: none -> 11.1 us  [local(): out = lax.dynamic_update_slice_in_dim(out, held, holder * extent, axis=0)]
  transfers between devices with their start and end apart: 6 -> 8, of which waited for: 6 -> 8; matrix products, arithmetic and copies ran while one was open for 1% -> 3% of each run, Pallas kernels for 0% -> 0%
where the time goes in v1:
time: 732 us; the launch traced here: 731 us
  waiting for transfers between devices  536 us (73%)
  blocking collectives  73.7 us (10%)
  local copies, waits for them, and re-layouts  46.3 us (6%)
  matrix products  37.4 us (5%)
  between operations  13.3 us (2%)
  other arithmetic  13.2 us (2%)
  starting transfers between devices  11.8 us (2%)
    reduce_scatter x1, waiting for transfers between devices, local(): lax.psum_scatter(partial_rows.reshape(experts * lax.axis_size('exp'), cap...  213 us
    ppermute x3, waiting for transfers between devices, local(): held = lax.ppermute(held, 'exp', ahead)  184 us
    all_to_all x1, blocking collectives, local(): lax.all_to_all(outgoing, ('ctx', 'head'), split_axis=0, concat_axis=0, ti...  73.7 us
    all_to_all x1, waiting for transfers between devices, local(): lax.all_to_all(summed, ('ctx', 'head'), split_axis=0, concat_axis=0, tile...  68.6 us
    all_gather x1, waiting for transfers between devices, local(): lax.all_gather(out_projection, 'exp', axis=1, tiled=True)  61 us
  transfers between devices with their start and end apart: 8, of which 8 were waited for; matrix products, arithmetic and copies ran while one was open for 3% of the time, Pallas kernels for 0%

profile of v1, /device:TPU:0, one launch (start us, length us, event | category | flops | bytes accessed | tf_op | source)
XLA Modules:
  0.0 731.1 jit_solution(11445882959898797913)
XLA Ops:
  6.5 0.0 copy-start
  6.5 0.0 all-gather.2.cloned.1.call-start
  6.5 0.7 all-gather.2.cloned.1.call-update
  7.3 0.0 reduce-scatter.3.cloned.1.call-start
  7.3 0.8 constant_dynamic-update-slice_fusion.1
  8.1 0.8 constant_dynamic-update-slice_fusion
  8.8 4.9 collective-permute-start
  13.8 0.1 fusion.18
  13.9 1.1 copy.19
  15.0 0.6 collective-permute-done
  15.6 0.1 copy.18
  15.7 0.1 copy.17
  15.8 0.8 fusion.29
  16.6 1.1 convolution_convert_fusion
  17.7 61.0 %all-gather.2.cloned.1.call-done = bf16[1024,2880]{0,1:T(8,128)(2,1)} async-done(((bf16[1024,720]{0,1:T(8,128)(2,1)}), bf16[1024,2880]{0,1:T(8,128)(2,1)}) %all-gather.2.cloned.1.call-update) | async-done | bytes 5898256 | tf_op jit(solution)/shard_map/all_gather | solution.py:95
  78.7 6.0 fusion.30
  84.7 0.0 reduce-scatter.3.cloned.1.call-update
  84.7 0.0 reduce-scatter.5.cloned.1.call-start
  84.8 0.0 copy-done.9
  84.8 0.1 copy.22
  84.9 0.1 eq.34
  85.0 0.1 eq.30
  85.1 0.6 reduce-window.6
  85.7 0.2 slice_reduce_fusion
  85.9 0.1 copy.21
  86.0 0.1 mul.91
  86.1 0.1 fusion.21
  86.2 7.6 %reduce-scatter.3.cloned.1.call-done = f32[64,2880]{1,0:T(8,128)} async-done(((f32[128,2880]{1,0:T(8,128)}), f32[64,2880]{1,0:T(8,128)}) %reduce-scatter.3.cloned.1.call-update) | async-done | bytes 737296 | tf_op jit(solution)/shard_map/reduce_scatter | solution.py:98
  93.8 0.0 copy-done.5
  93.8 1.3 multiply_reduce_fusion.1
  95.2 0.0 copy-done.8
  95.2 1.3 multiply_convert_fusion.1
  96.4 1.5 broadcast_in_dim.42
  98.0 3.6 reshape.129
  101.5 5.6 scatter_custom_fusion
  107.1 73.7 %all_to_all.10 = bf16[8,64,2880]{2,1,0:T(8,128)(2,1)S(1)} all-to-all(bf16[8,64,2880]{2,1,0:T(8,128)(2,1)} %bitcast.63), channel_id=1, replica_groups=mesh['ctx'=4,'exp'=4,'head'=2] {'ctx','head'}, dimensions={0} | all-to-all | bytes 5898240 | tf_op jit(solution)/shard_map/all_to_all | solution.py:118
  180.8 1.6 copy-done.2
  182.4 1.5 collective-permute-start.1
  183.9 66.3 %collective-permute-done.1 = bf16[8,64,2880]{2,1,0:T(8,128)(2,1)S(1)} collective-permute-done((bf16[8,64,2880]{2,1,0:T(8,128)(2,1)S(1)}, bf16[8,64,2880]{2,1,0:T(8,128)(2,1)S(1)}, u32[]{:S(2)}, u32[]{:S(2)}) %collective-permute-start.1) | collective-permute-done | bytes 2949152 | tf_op jit(solution)/shard_map/ppermute | solution.py:127
  250.2 1.6 copy-done.6
  251.7 0.6 collective-permute-start.2
  252.3 66.4 %collective-permute-done.2 = bf16[8,64,2880]{2,1,0:T(8,128)(2,1)} collective-permute-done((bf16[8,64,2880]{2,1,0:T(8,128)(2,1)S(1)}, bf16[8,64,2880]{2,1,0:T(8,128)(2,1)}, u32[]{:S(2)}, u32[]{:S(2)}) %collective-permute-start.2) | collective-permute-done | bytes 2949152 | tf_op jit(solution)/shard_map/ppermute | solution.py:127
  318.7 0.0 collective-permute-start.3
  318.7 6.1 broadcast_in_dim.40
  324.8 0.0 copy-done.3
  324.8 1.8 constant_dynamic-update-slice_fusion.5
  326.6 1.1 copy-done.7
  327.8 1.8 constant_dynamic-update-slice_fusion.4
  329.6 3.7 constant_dynamic-update-slice_fusion.3
  333.3 51.8 %collective-permute-done.3 = bf16[8,64,2880]{2,1,0:T(8,128)(2,1)} collective-permute-done((bf16[8,64,2880]{2,1,0:T(8,128)(2,1)}, bf16[8,64,2880]{2,1,0:T(8,128)(2,1)}, u32[]{:S(2)}, u32[]{:S(2)}) %collective-permute-start.3) | collective-permute-done | bytes 2949152 | tf_op jit(solution)/shard_map/ppermute | solution.py:127
  385.1 3.7 constant_dynamic-update-slice_fusion.2
  388.8 10.8 %fusion.7 = f32[2048,384]{1,0:T(8,128)S(1)} fusion(bf16[2048,2880]{1,0:T(8,128)(2,1)} %bitcast.61, bf16[1,2880,384]{2,1,0:T(8,128)(2,1)S(1)} %copy-done.11), kind=kOutput, calls=%fused_computation.9 | convolution fusion | flops 4529848320 | bytes 17154048 | tf_op jit(solution)/shard_map/dot_general | solution.py:60
  399.6 7.4 %multiply_convert_fusion = bf16[2048,384]{1,0:T(8,128)(2,1)S(1)} fusion(f32[2048,384]{1,0:T(8,128)S(1)} %fusion.7, bf16[2048,2880]{1,0:T(8,128)(2,1)S(1)} %bitcast.62, bf16[1,2880,384]{2,1,0:T(8,128)(2,1)S(1)} %copy-done.12), kind=kOutput, calls=%fused_computation.3 | convolution fusion | flops 4536139776 | bytes 18726912 | tf_op jit(solution)/shard_map/dot_general | solution.py:59
  407.1 11.4 %fusion.1 = f32[32,64,2880]{2,1,0:T(8,128)} fusion(bf16[32,64,384]{2,1,0:T(8,128)(2,1)S(1)} %bitcast.64, bf16[1,384,2880]{1,2,0:T(8,128)(2,1)S(1)} %copy-done), kind=kOutput, calls=%fused_computation.5 | convolution fusion | flops 4529848320 | bytes 27377664 | tf_op jit(solution)/shard_map/dot_general | solution.py:62
  418.5 0.0 reduce-scatter.5.cloned.1.call-update
  418.5 212.6 %reduce-scatter.5.cloned.1.call-done = f32[8,64,2880]{2,1,0:T(8,128)} async-done(((f32[32,64,2880]{2,1,0:T(8,128)}), f32[8,64,2880]{2,1,0:T(8,128)}) %reduce-scatter.5.cloned.1.call-update) | async-done | bytes 5898256 | tf_op jit(solution)/shard_map/reduce_scatter | solution.py:132
  631.0 4.8 convert_element_type.48
  635.9 4.8 all-to-all-start.1
  640.7 0.1 copy.24
  640.8 68.6 %all-to-all-done.1 = bf16[8,64,2880]{2,1,0:T(8,128)(2,1)} async-done(((bf16[8,64,2880]{2,1,0:T(8,128)(2,1)}), bf16[8,64,2880]{2,1,0:T(8,128)(2,1)}, u32[]{:S(2)}, u32[]{:S(2)}) %all-to-all-start.1) | async-done | bytes 2949152 | tf_op jit(solution)/shard_map/all_to_all | solution.py:138
  709.4 6.4 gather_fusion
  715.8 3.9 reshape.116
  719.7 4.0 multiply_reduce_fusion
  723.8 0.9 add_convert_fusion
  (29 shorter events, 0.1 us)
Async XLA Ops:
  6.5 400.5 %copy-start = (bf16[1,384,2880]{1,2,0:T(8,128)(2,1)S(1)}, bf16[1,384,2880]{1,2,0:T(8,128)(2,1)}, u32[]{:S(2)}) copy-start(bf16[1,384,2880]{1,2,0:T(8,128)(2,1)} %param.21) | copy-start | bytes 6635524
  6.5 72.2 %all-gather.2.cloned.1.call-start = ((), (), s32[]{:S(2)}) async-start(), calls=%async_computation.4 | async-start | bytes 7372800 | tf_op jit(solution)/shard_map/all_gather | solution.py:95
  7.3 86.6 %reduce-scatter.3.cloned.1.call-start = ((), (), s32[]{:S(2)}) async-start(), calls=%async_computation.5 | async-start | bytes 2260992 | tf_op jit(solution)/shard_map/reduce_scatter | solution.py:98
  8.8 6.8 collective-permute-start
  78.7 6.1 copy-start.9
  78.7 15.1 %copy-start.5 = (bf16[64,2880]{1,0:T(8,128)(2,1)S(1)}, bf16[64,2880]{1,0:T(8,128)(2,1)}, u32[]{:S(2)}) copy-start(bf16[64,2880]{1,0:T(8,128)(2,1)} %param.14) | copy-start | bytes 1105924
  78.7 16.5 %copy-start.8 = (f32[2880]{0:T(1024)S(1)}, f32[2880]{0:T(1024)}, u32[]{:S(2)}) copy-start(f32[2880]{0:T(1024)} %param.16) | copy-start | bytes 34564
  84.7 546.3 %reduce-scatter.5.cloned.1.call-start = ((), (), s32[]{:S(2)}) async-start(), calls=%async_computation.6 | async-start | bytes 30146560 | tf_op jit(solution)/shard_map/reduce_scatter | solution.py:132
  180.8 1.6 copy-start.2
  182.4 67.7 %collective-permute-start.1 = (bf16[8,64,2880]{2,1,0:T(8,128)(2,1)S(1)}, bf16[8,64,2880]{2,1,0:T(8,128)(2,1)S(1)}, u32[]{:S(2)}, u32[]{:S(2)}) collective-permute-start(bf16[8,64,2880]{2,1,0:T(8,128)(2,1)S(1)} %all_to_all.10), channel_id=1, source_target_pairs={{0,2},{2,4},{4,6},{6,0},{1,3},{3,5},{5,7},{7,1},{8,10},{10,12},{12... | collective-permute-start | bytes 8847368 | tf_op jit(solution)/shard_map/ppermute | solution.py:127
  250.2 1.6 copy-start.6
  251.7 67.0 %collective-permute-start.2 = (bf16[8,64,2880]{2,1,0:T(8,128)(2,1)S(1)}, bf16[8,64,2880]{2,1,0:T(8,128)(2,1)}, u32[]{:S(2)}, u32[]{:S(2)}) collective-permute-start(bf16[8,64,2880]{2,1,0:T(8,128)(2,1)S(1)} %collective-permute-done.1), channel_id=1, source_target_pairs={{0,2},{2,4},{4,6},{6,0},{1,3},{3,5},{5,7},{7,1},{8,10},{10,12},{12... | collective-permute-start | bytes 8847368 | tf_op jit(solution)/shard_map/ppermute | solution.py:127
  318.7 66.3 %collective-permute-start.3 = (bf16[8,64,2880]{2,1,0:T(8,128)(2,1)}, bf16[8,64,2880]{2,1,0:T(8,128)(2,1)}, u32[]{:S(2)}, u32[]{:S(2)}) collective-permute-start(bf16[8,64,2880]{2,1,0:T(8,128)(2,1)} %collective-permute-done.2), channel_id=1, source_target_pairs={{0,2},{2,4},{4,6},{6,0},{1,3},{3,5},{5,7},{7,1},{8,10},{10,12},{12... | collective-permute-start | bytes 8847368 | tf_op jit(solution)/shard_map/ppermute | solution.py:127
  318.7 6.1 copy-start.3
  324.8 2.9 copy-start.7
  333.3 55.5 %copy-start.11 = (bf16[1,2880,384]{2,1,0:T(8,128)(2,1)S(1)}, bf16[1,2880,384]{2,1,0:T(8,128)(2,1)}, u32[]{:S(2)}) copy-start(bf16[1,2880,384]{2,1,0:T(8,128)(2,1)} %param.20) | copy-start | bytes 6635524
  388.8 10.8 %copy-start.1 = (bf16[32,64,2880]{2,1,0:T(8,128)(2,1)S(1)}, bf16[32,64,2880]{2,1,0:T(8,128)(2,1)}, u32[]{:S(2)}) copy-start(bf16[32,64,2880]{2,1,0:T(8,128)(2,1)} %constant_dynamic-update-slice_fusion.2) | copy-start | bytes 35389444
  388.8 10.8 %copy-start.12 = (bf16[1,2880,384]{2,1,0:T(8,128)(2,1)S(1)}, bf16[1,2880,384]{2,1,0:T(8,128)(2,1)}, u32[]{:S(2)}) copy-start(bf16[1,2880,384]{2,1,0:T(8,128)(2,1)} %param.19) | copy-start | bytes 6635524
  635.9 4.8 copy-start.10
  635.9 73.5 %all-to-all-start.1 = ((bf16[8,64,2880]{2,1,0:T(8,128)(2,1)}), bf16[8,64,2880]{2,1,0:T(8,128)(2,1)}, u32[]{:S(2)}, u32[]{:S(2)}) async-start(bf16[8,64,2880]{2,1,0:T(8,128)(2,1)} %convert_element_type.48), calls=%async_computation.3 | async-start | bytes 6029312 | tf_op jit(solution)/shard_map/all_to_all | solution.py:138
  719.7 4.0 copy-start.4
Sparse Core Ops, SparseCore 0:
  9.2 69.4 all-gather.1
  84.8 8.9 reduce-scatter.2
  418.6 212.3 reduce-scatter.4
